TPU v7x, 512 devices: a whole 4x4x16 slice. The times are simulated.
512 devices in a mesh: batch: 64 (over z, y_hi, core), coef: 8 (over y_lo, x).
Axes of the slice: x: 4, y: 4 (y_hi: 2, y_lo: 2; y = y_hi * 2 + y_lo), z: 16, core: 2. Of those that a mesh axis runs over, the one named last changes fastest.
Arguments:
- jac_blocks: bfloat16 [2048, 8, 2, 128, 128], P(('batch', 'coef')), may hold values from -0.52734375 to 0.52734375
- col_blocks: int32 [8, 2048, 2], P('coef', 'batch'), may hold values from 0 to 63, all different within a row; in each aligned block of 32 rows (0 to 31, 32 to 63, ..., all dimensions but the last counted through in order) at most 2 rows name the same one
- residual: float32 [2048, 128], P('batch'), may hold values from -6 to 6
- run_of_half: int32 [4096], P('batch'), may hold values from 0 to 4095, each once
- run_scale: bfloat16 [4096], replicated, may hold values from 0.25 to 4
Outputs:
- diag_blocks: float32 [8, 64, 128, 128], P('coef', 'batch')
- gradient: float32 [8, 64, 128], P('coef', 'batch')
Inputs may be any that keep to these rules, and one draw needn't show every extreme that they name: `col_blocks`: the 2 column blocks of one row block in one group differ. For each group, among the row blocks of one batch index (aligned blocks of the row-block dimension), no column block is named more than 2 times, a bound that some block reaches. `run_of_half`: every run appears exactly once.
All inputs are finite; a program needn't handle non-finite values.
Results may differ from a plain program's by a relative error of at most 0.00043.
Values may be sent and summed in bfloat16 or wider, within the bound.
No kernel may reach another device: no remote copies, remote signals or barrier semaphores. Data moves between devices by JAX's collectives and lax.ppermute only.
A program may use at most 64 MiB of HBM per device.

v0:
```python
import jax
import jax.numpy as jnp
from jax import lax
from jax.sharding import PartitionSpec as P

BS = 128
PAIR = 2


def shards(jac_blocks, col_blocks, residual, run_of_half, run_scale):
    width = lax.axis_size("batch")
    myself = lax.axis_index("batch")
    moved = lax.all_to_all(jac_blocks, "coef", split_axis=1, concat_axis=0, tiled=True)
    items = moved.reshape(-1, BS, BS)
    targets = col_blocks.reshape(-1)
    scale_rows = run_scale.astype(jnp.float32)[run_of_half].reshape(-1, 2)
    weights = jnp.repeat(scale_rows, BS // 2, axis=1)
    item_w = jnp.repeat(weights, PAIR, axis=0)
    item_res = jnp.repeat(residual, PAIR, axis=0)
    onehot = (targets[:, None] == jnp.arange(width, dtype=jnp.int32)[None, :]).astype(jnp.float32)
    gterms = jnp.einsum(
        "iak,ia->ik", items.astype(jnp.float32), item_w * item_res, precision=lax.Precision.HIGHEST
    )
    gpart = jnp.einsum("il,ik->lk", onehot, gterms, precision=lax.Precision.HIGHEST)
    gtotal = lax.psum(gpart, "batch")
    gradient = lax.dynamic_slice_in_dim(gtotal, myself, 1, 0).reshape(1, 1, BS)
    weighted = (items.astype(jnp.float32) * item_w[:, :, None]).astype(jnp.bfloat16)
    products = lax.dot_general(
        items, weighted, (((1,), (1,)), ((0,), (0,))), preferred_element_type=jnp.float32
    )
    diag = lax.psum_scatter(
        jnp.einsum("il,ikb->lkb", onehot, products, precision=lax.Precision.HIGHEST),
        "batch",
        scatter_dimension=0,
        tiled=True,
    )
    return (diag.reshape(1, 1, BS, BS), gradient)


def solution(mesh):
    in_specs = (
        P(("batch", "coef"), None, None, None, None),
        P("coef", "batch", None),
        P("batch", None),
        P("batch"),
        P(),
    )
    out_specs = (P("coef", "batch", None, None), P("coef", "batch", None))
    return jax.shard_map(shards, mesh=mesh, in_specs=in_specs, out_specs=out_specs, check_vma=False)
```

profile of v0, /device:TPU:6, one launch (start us, length us, event | category | flops | bytes accessed | tf_op | source)
XLA Modules:
  0.0 338.0 jit_solution(15510032029880882865)
XLA Ops:
  7.2 0.0 copy-start.2
  7.2 0.0 copy-start.1
  7.2 0.0 copy-start.3
  7.2 3.2 copy.11
  10.4 9.4 %all-to-all-start = ((bf16[4,8,2,128,128]{4,3,2,0,1:T(8,128)(2,1)}), bf16[4,8,2,128,128]{4,3,2,0,1:T(8,128)(2,1)S(1)}, u32[]{:S(2)}, u32[]{:S(2)}) async-start(bf16[4,8,2,128,128]{4,3,2,0,1:T(8,128)(2,1)} %copy.11), calls=%async_computation | async-start | bytes 4194304 | tf_op jit(solution)/shard_map/all_to_all | solution.py:13
  19.8 0.0 reduce-scatter.2.cloned.1.call-start
  19.8 0.0 copy-done.2
  19.8 0.1 copy.10
  19.8 0.1 eq.15
  20.0 0.0 copy-done.1
  20.0 0.0 copy-done.3
  20.0 0.8 gather_fusion
  20.8 0.1 reshape.27
  20.9 0.1 broadcast_in_dim.14
  21.0 0.1 reshape.28
  21.1 20.6 %all-to-all-done = bf16[4,8,2,128,128]{4,3,2,0,1:T(8,128)(2,1)S(1)} async-done(((bf16[4,8,2,128,128]{4,3,2,0,1:T(8,128)(2,1)}), bf16[4,8,2,128,128]{4,3,2,0,1:T(8,128)(2,1)S(1)}, u32[]{:S(2)}, u32[]{:S(2)}) %all-to-all-start) | async-done | bytes 2097184 | tf_op jit(solution)/shard_map/all_to_all | solution.py:13
  41.7 4.2 %fusion.1 = f32[64,128,128]{1,2,0:T(8,128)} fusion(bf16[64,128,128]{2,1,0:T(8,128)(2,1)S(1)} %bitcast.25, f32[64,128]{1,0:T(8,128)S(1)} %bitcast.27), kind=kOutput, calls=%fused_computation.3 | convolution fusion | flops 271581184 | bytes 6324224 | tf_op jit(solution)/shard_map/dot_general | solution.py:28
  45.8 5.4 %copy.13 = f32[64,128,128]{2,0,1:T(8,128)} copy(f32[64,128,128]{1,2,0:T(8,128)} %fusion.1) | data formatting | bytes 8388608 | tf_op jit(solution)/shard_map/dot_general | solution.py:28
  51.2 4.6 %fusion.5 = f32[64,128,128]{2,0,1:T(8,128)S(1)} fusion(f32[64,128,128]{2,0,1:T(8,128)} %copy.13, s32[64]{0:T(128)S(1)} %eq.15), kind=kOutput, calls=%fused_computation.8 | convolution fusion | flops 805310464 | bytes 8388864 | tf_op jit(solution)/shard_map/il,ikb->lkb/dot_general | solution.py:32
  55.8 4.4 %copy.14 = f32[64,128,128]{2,1,0:T(8,128)} copy(f32[64,128,128]{2,0,1:T(8,128)S(1)} %fusion.5) | data formatting | bytes 8388608 | tf_op jit(solution)/shard_map/il,ikb->lkb/dot_general | solution.py:32
  60.2 0.0 copy-start
  60.2 0.0 reduce-scatter.2.cloned.1.call-update
  60.2 0.7 copy-done
  60.9 1.7 fusion.9
  62.7 0.1 fusion.3
  62.8 267.8 %psum.7 = f32[64,128]{1,0:T(8,128)S(1)} all-reduce(f32[64,128]{1,0:T(8,128)S(1)} %fusion.3), channel_id=1, replica_groups=mesh['batch'=64,'coef'=8] {'batch'}, use_global_device_ids=true, to_apply=%region_1.0 | all-reduce | flops 8192 | bytes 65536 | tf_op jit(solution)/shard_map/psum | solution.py:25
  330.7 0.5 dynamic-slice_bitcast_fusion
  331.2 0.0 reduce-scatter.2.cloned.1.call-done
  (6 shorter events, 0.0 us)
Async XLA Ops:
  7.2 12.6 %copy-start.2 = (s32[1,32,2]{1,2,0:T(2,128)S(1)}, s32[1,32,2]{1,2,0:T(2,128)}, u32[]{:S(2)}) copy-start(s32[1,32,2]{1,2,0:T(2,128)} %param.6) | copy-start | bytes 772
  7.2 12.8 %copy-start.1 = (bf16[4096]{0:T(1024)(128)(2,1)S(1)}, bf16[4096]{0:T(1024)(128)(2,1)}, u32[]{:S(2)}) copy-start(bf16[4096]{0:T(1024)(128)(2,1)} %param.9) | copy-start | bytes 24580
  7.2 12.8 %copy-start.3 = (s32[64]{0:T(128)S(1)}, s32[64]{0:T(128)}, u32[]{:S(2)}) copy-start(s32[64]{0:T(128)} %param.8) | copy-start | bytes 772
  10.4 31.3 %all-to-all-start = ((bf16[4,8,2,128,128]{4,3,2,0,1:T(8,128)(2,1)}), bf16[4,8,2,128,128]{4,3,2,0,1:T(8,128)(2,1)S(1)}, u32[]{:S(2)}, u32[]{:S(2)}) async-start(bf16[4,8,2,128,128]{4,3,2,0,1:T(8,128)(2,1)} %copy.11), calls=%async_computation | async-start | bytes 4194304 | tf_op jit(solution)/shard_map/all_to_all | solution.py:13
  19.8 311.4 %reduce-scatter.2.cloned.1.call-start = ((), (), s32[]{:S(2)}) async-start(), calls=%async_computation.2 | async-start | bytes 4259840 | tf_op jit(solution)/shard_map/reduce_scatter | solution.py:31
  60.2 0.7 copy-start
Sparse Core Ops, SparseCore 0:
  60.3 228.2 reduce-scatter.1
where the time goes:
time: 338 us
  blocking collectives  268 us (79%)
  waiting for transfers between devices  20.6 us (6%)
  local copies, waits for them, and re-layouts  15.5 us (5%)
  between operations  14.1 us (4%)
  matrix products  10.6 us (3%)
  starting transfers between devices  9.37 us (3%)
    psum x1, blocking collectives, shards(): gtotal = lax.psum(gpart, 'batch')  268 us
    all_to_all x1, waiting for transfers between devices, shards(): lax.all_to_all(jac_blocks, 'coef', split_axis=1, concat_axis=0, tiled=True)  20.6 us
    all_to_all x1, starting transfers between devices, shards(): lax.all_to_all(jac_blocks, 'coef', split_axis=1, concat_axis=0, tiled=True)  9.37 us
  transfers between devices with their start and end apart: 2, of which 1 were waited for; matrix products, arithmetic and copies ran while one was open for 1% of the time, Pallas kernels for 0%

commit v1 on v0

--- a/solution.py
+++ b/solution.py
@@ -22,7 +22,7 @@
         "iak,ia->ik", items.astype(jnp.float32), item_w * item_res, precision=lax.Precision.HIGHEST
     )
     gpart = jnp.einsum("il,ik->lk", onehot, gterms, precision=lax.Precision.HIGHEST)
-    gtotal = lax.psum(gpart, "batch")
+    gtotal = jnp.sum(lax.all_gather(gpart, "batch"), axis=0)
     gradient = lax.dynamic_slice_in_dim(gtotal, myself, 1, 0).reshape(1, 1, BS)
     weighted = (items.astype(jnp.float32) * item_w[:, :, None]).astype(jnp.bfloat16)
     products = lax.dot_general(

time: 338 us -> 423 us (1.25)
  waiting for transfers between devices: 20.6 us -> 371 us
  blocking collectives: 268 us -> 0 us
    psum x1 -> x0, blocking collectives: 268 us -> none  [shards(): gtotal = lax.psum(gpart, 'batch')]
    reduce_scatter x1, waiting for transfers between devices: 0.01 us -> 219 us  [shards(): lax.psum_scatter(jnp.einsum('il,ikb->lkb', onehot, products, precision=la...]
    all_gather x0 -> x1, waiting for transfers between devices: none -> 131 us  [shards(): gtotal = jnp.sum(lax.all_gather(gpart, 'batch'), axis=0)]
  transfers between devices with their start and end apart: 2 -> 3, of which waited for: 1 -> 3; matrix products, arithmetic and copies ran while one was open for 1% -> 5% of each run, Pallas kernels for 0% -> 0%
where the time goes in v1:
time: 423 us
  waiting for transfers between devices  371 us (88%)
  local copies, waits for them, and re-layouts  14.8 us (3%)
  between operations  14.1 us (3%)
  matrix products  11.2 us (3%)
  starting transfers between devices  9.56 us (2%)
    reduce_scatter x1, waiting for transfers between devices, shards(): lax.psum_scatter(jnp.einsum('il,ikb->lkb', onehot, products, precision=la...  219 us
    all_gather x1, waiting for transfers between devices, shards(): gtotal = jnp.sum(lax.all_gather(gpart, 'batch'), axis=0)  131 us
    all_to_all x1, waiting for transfers between devices, shards(): lax.all_to_all(jac_blocks, 'coef', split_axis=1, concat_axis=0, tiled=True)  20.5 us
    all_to_all x1, starting transfers between devices, shards(): lax.all_to_all(jac_blocks, 'coef', split_axis=1, concat_axis=0, tiled=True)  9.51 us
  transfers between devices with their start and end apart: 3, of which 3 were waited for; matrix products, arithmetic and copies ran while one was open for 5% of the time, Pallas kernels for 0%

profile of v1, /device:TPU:6, one launch (start us, length us, event | category | flops | bytes accessed | tf_op | source)
XLA Modules:
  0.0 422.6 jit_solution(3361974276298030179)
XLA Ops:
  7.2 3.2 copy.11
  10.4 0.0 copy-start.2
  10.4 0.0 copy-start.1
  10.4 0.0 copy-start.3
  10.4 0.0 copy-start
  10.4 9.5 %all-to-all-start = ((bf16[4,8,2,128,128]{4,3,2,0,1:T(8,128)(2,1)}), bf16[4,8,2,128,128]{4,3,2,0,1:T(8,128)(2,1)S(1)}, u32[]{:S(2)}, u32[]{:S(2)}) async-start(bf16[4,8,2,128,128]{4,3,2,0,1:T(8,128)(2,1)} %copy.11), calls=%async_computation | async-start | bytes 4194304 | tf_op jit(solution)/shard_map/all_to_all | solution.py:13
  19.9 0.0 all-gather.3.cloned.1.call-start
  19.9 0.0 copy-done.2
  19.9 0.1 copy.10
  20.0 0.1 eq.15
  20.1 0.0 copy-done.1
  20.1 0.0 copy-done.3
  20.1 0.8 gather_fusion
  20.9 0.1 reshape.27
  21.0 0.1 broadcast_in_dim.14
  21.1 0.1 reshape.28
  21.2 0.0 copy-done
  21.3 20.5 %all-to-all-done = bf16[4,8,2,128,128]{4,3,2,0,1:T(8,128)(2,1)S(1)} async-done(((bf16[4,8,2,128,128]{4,3,2,0,1:T(8,128)(2,1)}), bf16[4,8,2,128,128]{4,3,2,0,1:T(8,128)(2,1)S(1)}, u32[]{:S(2)}, u32[]{:S(2)}) %all-to-all-start) | async-done | bytes 2097184 | tf_op jit(solution)/shard_map/all_to_all | solution.py:13
  41.8 1.7 fusion.9
  43.5 0.8 fusion.3
  44.3 0.0 all-gather.3.cloned.1.call-update
  44.3 0.0 reduce-scatter.2.cloned.1.call-start
  44.4 4.1 fusion.1
  48.5 5.4 %copy.13 = f32[64,128,128]{2,0,1:T(8,128)} copy(f32[64,128,128]{1,2,0:T(8,128)} %fusion.1) | data formatting | bytes 8388608 | tf_op jit(solution)/shard_map/dot_general | solution.py:28
  53.9 4.6 %fusion.5 = f32[64,128,128]{2,0,1:T(8,128)S(1)} fusion(f32[64,128,128]{2,0,1:T(8,128)} %copy.13, s32[64]{0:T(128)S(1)} %eq.15), kind=kOutput, calls=%fused_computation.8 | convolution fusion | flops 805310464 | bytes 8388864 | tf_op jit(solution)/shard_map/il,ikb->lkb/dot_general | solution.py:32
  58.5 4.4 %copy.14 = f32[64,128,128]{2,1,0:T(8,128)} copy(f32[64,128,128]{2,0,1:T(8,128)S(1)} %fusion.5) | data formatting | bytes 8388608 | tf_op jit(solution)/shard_map/il,ikb->lkb/dot_general | solution.py:32
  62.9 0.0 reduce-scatter.2.cloned.1.call-update
  62.9 131.1 %all-gather.3.cloned.1.call-done = f32[4096,128]{1,0:T(8,128)} async-done(((f32[64,128]{1,0:T(8,128)}), f32[4096,128]{1,0:T(8,128)}) %all-gather.3.cloned.1.call-update) | async-done | bytes 2097168 | tf_op jit(solution)/shard_map/all_gather | solution.py:25
  194.0 1.7 reduce_sum.9
  195.8 0.5 dynamic-slice_bitcast_fusion
  196.3 219.5 %reduce-scatter.2.cloned.1.call-done = f32[1,128,128]{2,1,0:T(8,128)} async-done(((f32[64,128,128]{2,1,0:T(8,128)}), f32[1,128,128]{2,1,0:T(8,128)}) %reduce-scatter.2.cloned.1.call-update) | async-done | bytes 65552 | tf_op jit(solution)/shard_map/reduce_scatter | solution.py:31
  (6 shorter events, 0.0 us)
Async XLA Ops:
  10.4 9.5 %copy-start.2 = (s32[1,32,2]{1,2,0:T(2,128)S(1)}, s32[1,32,2]{1,2,0:T(2,128)}, u32[]{:S(2)}) copy-start(s32[1,32,2]{1,2,0:T(2,128)} %param.6) | copy-start | bytes 772
  10.4 9.7 %copy-start.1 = (bf16[4096]{0:T(1024)(128)(2,1)S(1)}, bf16[4096]{0:T(1024)(128)(2,1)}, u32[]{:S(2)}) copy-start(bf16[4096]{0:T(1024)(128)(2,1)} %param.9) | copy-start | bytes 24580
  10.4 9.7 %copy-start.3 = (s32[64]{0:T(128)S(1)}, s32[64]{0:T(128)}, u32[]{:S(2)}) copy-start(s32[64]{0:T(128)} %param.8) | copy-start | bytes 772
  10.4 10.9 %copy-start = (f32[32,128]{1,0:T(8,128)S(1)}, f32[32,128]{1,0:T(8,128)}, u32[]{:S(2)}) copy-start(f32[32,128]{1,0:T(8,128)} %param.7) | copy-start | bytes 49156
  10.4 31.4 %all-to-all-start = ((bf16[4,8,2,128,128]{4,3,2,0,1:T(8,128)(2,1)}), bf16[4,8,2,128,128]{4,3,2,0,1:T(8,128)(2,1)S(1)}, u32[]{:S(2)}, u32[]{:S(2)}) async-start(bf16[4,8,2,128,128]{4,3,2,0,1:T(8,128)(2,1)} %copy.11), calls=%async_computation | async-start | bytes 4194304 | tf_op jit(solution)/shard_map/all_to_all | solution.py:13
  19.9 174.2 %all-gather.3.cloned.1.call-start = ((), (), s32[]{:S(2)}) async-start(), calls=%async_computation.3 | async-start | bytes 2129920 | tf_op jit(solution)/shard_map/all_gather | solution.py:25
  44.3 371.5 %reduce-scatter.2.cloned.1.call-start = ((), (), s32[]{:S(2)}) async-start(), calls=%async_computation.2 | async-start | bytes 4259840 | tf_op jit(solution)/shard_map/reduce_scatter | solution.py:31
Sparse Core Ops, SparseCore 0:
  44.4 149.5 all-gather.2
  199.3 216.4 reduce-scatter.1
